TPU v7x, 32 devices: a whole 2x2x4 slice. The times are simulated.
32 devices in a mesh: dp: 8 (over y, x, core), fsdp: 4 (over z).
Axes of the slice: x: 2, y: 2, z: 4, core: 2. Of those that a mesh axis runs over, the one named last changes fastest.
Arguments:
- tokens: bfloat16 [32, 256, 1152], P(('dp', 'fsdp')), may hold values from -6 to 6
- condition: bfloat16 [32, 1152], P(('dp', 'fsdp')), may hold values from -6 to 6
- grid_sizes: int32 [32, 2], P(('dp', 'fsdp')), may hold values from 12 to 20, as said below
- w_ada: bfloat16 [1152, 6912], P('fsdp'), may hold values from -0.1875 to 0.1875
- w_qkv: bfloat16 [1152, 3456], P('fsdp'), may hold values from -0.1875 to 0.1875
- w_out: bfloat16 [1152, 1152], P('fsdp'), may hold values from -1 to 1
- w_up: bfloat16 [1152, 4608], P('fsdp'), may hold values from -0.1875 to 0.1875
- w_down: bfloat16 [4608, 1152], P('fsdp'), may hold values from -0.09375 to 0.09375
- b_ada: bfloat16 [6912], P('fsdp'), may hold values from -3 to 3
- b_qv: bfloat16 [2304], P('fsdp'), may hold values from -3 to 3
- b_out: bfloat16 [1152], P('fsdp'), may hold values from -3 to 3
- b_up: bfloat16 [4608], P('fsdp'), may hold values from -3 to 3
- b_down: bfloat16 [1152], P('fsdp'), may hold values from -3 to 3
- cotangent: bfloat16 [32, 256, 1152], P(('dp', 'fsdp')), may hold values from -6 to 6
Outputs:
- output: bfloat16 [32, 256, 1152], P(('dp', 'fsdp'))
- grad_tokens: bfloat16 [32, 256, 1152], P(('dp', 'fsdp'))
- grad_condition: float32 [32, 1152], P(('dp', 'fsdp'))
- grad_w_ada: float32 [1152, 6912], P('fsdp', 'dp')
- grad_w_qkv: float32 [1152, 3456], P('fsdp', 'dp')
- grad_w_out: float32 [1152, 1152], P('fsdp', 'dp')
- grad_w_up: float32 [1152, 4608], P('fsdp', 'dp')
- grad_w_down: float32 [4608, 1152], P('fsdp', 'dp')
- grad_b_ada: float32 [6912], P('fsdp')
- grad_b_qv: float32 [2304], P('fsdp')
- grad_b_out: float32 [1152], P('fsdp')
- grad_b_up: float32 [4608], P('fsdp')
- grad_b_down: float32 [1152], P('fsdp')
Inputs may be any that keep to these rules, and one draw needn't show every extreme that they name: `grid_sizes`: each image grid has 12 to 20 rows and columns and at most 256 tokens; image 0 has 12 rows and 20 columns, and image 1 has 20 rows and 12 columns.
All inputs are finite; a program needn't handle non-finite values.
Results may differ from a plain program's by a relative error of at most 0.015.
The roundings to bfloat16 on the way count: a program that leaves them out, or rounds other values in their place, can miss the bound.
Values may be sent and summed in bfloat16 or wider, within the bound.
No kernel may reach another device: no remote copies, remote signals or barrier semaphores. Data moves between devices by JAX's collectives and lax.ppermute only.
A program may use at most 256 MiB of HBM per device.

v0:
```python
import math
import jax
import jax.numpy as jnp
from jax import lax
from jax.sharding import PartitionSpec as P

HEAD_DIM = 72
epsilon = 1e-06
masked_value = -1e30
gelu_root = math.sqrt(2.0 / math.pi)


def layer_norm(values_in):
    centred = values_in - jnp.mean(values_in, axis=-1, keepdims=True)
    spread = jnp.mean(centred * centred, axis=-1, keepdims=True)
    return centred * lax.rsqrt(spread + epsilon)


def gelu_tanh(pre_act):
    return (
        0.5
        * pre_act
        * (1.0 + jnp.tanh(gelu_root * (pre_act + 0.044715 * pre_act * pre_act * pre_act)))
    )


def apply_rows(left, right):
    return jnp.einsum("isd,de->ise", left, right, preferred_element_type=jnp.float32)


def forward_pass(weights_full, tokens_wide, cond_act, live_keys, kept_lse):
    w_ada, w_qkv, w_out, w_up, w_down, b_ada, b_qv, b_out, b_up, b_down = weights_full
    width = w_out.shape[0]
    images = tokens_wide.shape[0]
    slots = tokens_wide.shape[1]
    heads = width // HEAD_DIM
    modulation = jnp.dot(cond_act, w_ada, preferred_element_type=jnp.float32) + b_ada.astype(
        jnp.float32
    )
    portions = jnp.split(modulation, 6, axis=1)
    modulated = tuple((portion[:, None, :] for portion in portions))
    shift_one, scale_one, gate_one, shift_two, scale_two, gate_two = modulated
    norm_one = layer_norm(tokens_wide)
    normed = (norm_one * (1.0 + scale_one) + shift_one).astype(jnp.bfloat16)
    projected = apply_rows(normed, w_qkv)
    bias_qv = b_qv.astype(jnp.float32)
    queries = (
        (projected[..., :width] + bias_qv[:width])
        .astype(jnp.bfloat16)
        .reshape(images, slots, heads, HEAD_DIM)
    )
    key_part = (
        projected[..., width : 2 * width]
        .astype(jnp.bfloat16)
        .reshape(images, slots, heads, HEAD_DIM)
    )
    values = (
        (projected[..., 2 * width :] + bias_qv[width:])
        .astype(jnp.bfloat16)
        .reshape(images, slots, heads, HEAD_DIM)
    )
    raw = jnp.einsum(
        "iqhe,ikhe->ihqk", queries, key_part, preferred_element_type=jnp.float32
    ) * HEAD_DIM ** (-0.5)
    scores = jnp.where(live_keys[:, None, None, :], raw, masked_value)
    if kept_lse is None:
        highest = jnp.max(scores, axis=-1, keepdims=True)
        lse = highest + jnp.log(jnp.sum(jnp.exp(scores - highest), axis=-1, keepdims=True))
    else:
        lse = kept_lse
    probs = jnp.exp(scores - lse)
    probs_low = probs.astype(jnp.bfloat16)
    attended = jnp.einsum("ihqk,ikhe->iqhe", probs_low, values, preferred_element_type=jnp.float32)
    attended = attended.reshape(images, slots, width).astype(jnp.bfloat16)
    attn_out = apply_rows(attended, w_out) + b_out.astype(jnp.float32)
    middle = tokens_wide + gate_one * attn_out
    norm_two = layer_norm(middle)
    normed_two = (norm_two * (1.0 + scale_two) + shift_two).astype(jnp.bfloat16)
    pre_act = apply_rows(normed_two, w_up) + b_up.astype(jnp.float32)
    activated = gelu_tanh(pre_act).astype(jnp.bfloat16)
    mlp_out = apply_rows(activated, w_down) + b_down.astype(jnp.float32)
    return (
        modulated,
        norm_one,
        normed,
        queries,
        key_part,
        values,
        lse,
        probs,
        probs_low,
        attended,
        attn_out,
        middle,
        norm_two,
        normed_two,
        pre_act,
        activated,
        mlp_out,
    )


def body(
    tokens,
    condition,
    grid_sizes,
    w_ada,
    w_qkv,
    w_out,
    w_up,
    w_down,
    b_ada,
    b_qv,
    b_out,
    b_up,
    b_down,
    cotangent,
):
    weights_full = (
        lax.all_gather(w_ada, "fsdp", axis=0, tiled=True),
        lax.all_gather(w_qkv, "fsdp", axis=0, tiled=True),
        lax.all_gather(w_out, "fsdp", axis=0, tiled=True),
        lax.all_gather(w_up, "fsdp", axis=0, tiled=True),
        lax.all_gather(w_down, "fsdp", axis=0, tiled=True),
        lax.all_gather(b_ada, "fsdp", axis=0, tiled=True),
        lax.all_gather(b_qv, "fsdp", axis=0, tiled=True),
        lax.all_gather(b_out, "fsdp", axis=0, tiled=True),
        lax.all_gather(b_up, "fsdp", axis=0, tiled=True),
        lax.all_gather(b_down, "fsdp", axis=0, tiled=True),
    )
    images = tokens.shape[0]
    slots = tokens.shape[1]
    width = tokens.shape[2]
    heads = width // HEAD_DIM
    live_counts = grid_sizes[:, 0] * grid_sizes[:, 1]
    live_keys = lax.broadcasted_iota(jnp.int32, (images, slots), 1) < live_counts[:, None]
    live_rows = live_keys.astype(jnp.float32)[:, :, None]
    tokens_wide = tokens.astype(jnp.float32)
    cond_wide = condition.astype(jnp.float32)
    cond_act = (cond_wide * jax.nn.sigmoid(cond_wide)).astype(jnp.bfloat16)
    saved = forward_pass(weights_full, tokens_wide, cond_act, live_keys, None)
    middle_first = saved[11]
    gate_first = saved[0][5]
    mlp_first = saved[16]
    output = (live_rows * (middle_first + gate_first * mlp_first)).astype(jnp.bfloat16)
    weights_back = (
        lax.all_gather(w_ada, "fsdp", axis=0, tiled=True),
        lax.all_gather(w_qkv, "fsdp", axis=0, tiled=True),
        lax.all_gather(w_out, "fsdp", axis=0, tiled=True),
        lax.all_gather(w_up, "fsdp", axis=0, tiled=True),
        lax.all_gather(w_down, "fsdp", axis=0, tiled=True),
        lax.all_gather(b_ada, "fsdp", axis=0, tiled=True),
        lax.all_gather(b_qv, "fsdp", axis=0, tiled=True),
        lax.all_gather(b_out, "fsdp", axis=0, tiled=True),
        lax.all_gather(b_up, "fsdp", axis=0, tiled=True),
        lax.all_gather(b_down, "fsdp", axis=0, tiled=True),
    )
    saved = forward_pass(weights_back, tokens_wide, cond_act, live_keys, saved[6])
    (
        modulated,
        norm_one,
        normed,
        queries,
        key_part,
        values,
        lse,
        probs,
        probs_low,
        attended,
        attn_out,
        middle,
        norm_two,
        normed_two,
        pre_act,
        activated,
        mlp_out,
    ) = saved
    shift_one, scale_one, gate_one, shift_two, scale_two, gate_two = modulated
    ada_full, qkv_full, out_full, up_full, down_full = (
        weights_back[0],
        weights_back[1],
        weights_back[2],
        weights_back[3],
        weights_back[4],
    )
    upstream = live_rows * cotangent.astype(jnp.float32)
    d_gate_two = jnp.sum(upstream * mlp_out, axis=1)
    d_mlp = (gate_two * upstream).astype(jnp.bfloat16)
    grad_w_down = jnp.einsum("isf,isd->fd", activated, d_mlp, preferred_element_type=jnp.float32)
    grad_b_down = jnp.sum(d_mlp.astype(jnp.float32), axis=(0, 1))
    d_act = jnp.einsum("isd,fd->isf", d_mlp, down_full, preferred_element_type=jnp.float32)
    unused_gelu, gelu_pull = jax.vjp(gelu_tanh, pre_act)
    d_pre = gelu_pull(d_act)[0].astype(jnp.bfloat16)
    grad_w_up = jnp.einsum("isd,isf->df", normed_two, d_pre, preferred_element_type=jnp.float32)
    grad_b_up = jnp.sum(d_pre.astype(jnp.float32), axis=(0, 1))
    d_normed_two = jnp.einsum("isf,df->isd", d_pre, up_full, preferred_element_type=jnp.float32)
    d_shift_two = jnp.sum(d_normed_two, axis=1)
    d_scale_two = jnp.sum(d_normed_two * norm_two, axis=1)
    unused_norm, second_pull = jax.vjp(layer_norm, middle)
    d_middle = upstream + second_pull(d_normed_two * (1.0 + scale_two))[0]
    d_gate_one = jnp.sum(d_middle * attn_out, axis=1)
    d_attn = (gate_one * d_middle).astype(jnp.bfloat16)
    grad_w_out = jnp.einsum("isd,ise->de", attended, d_attn, preferred_element_type=jnp.float32)
    grad_b_out = jnp.sum(d_attn.astype(jnp.float32), axis=(0, 1))
    d_attended = jnp.einsum("ise,de->isd", d_attn, out_full, preferred_element_type=jnp.float32)
    d_attended = d_attended.astype(jnp.bfloat16).reshape(images, slots, heads, HEAD_DIM)
    d_probs = jnp.einsum("iqhe,ikhe->ihqk", d_attended, values, preferred_element_type=jnp.float32)
    d_values = jnp.einsum(
        "ihqk,iqhe->ikhe", probs_low, d_attended, preferred_element_type=jnp.float32
    ).astype(jnp.bfloat16)
    row_inner = jnp.sum(probs * d_probs, axis=-1, keepdims=True)
    d_scores = (probs * (d_probs - row_inner)).astype(jnp.bfloat16)
    d_queries = (
        jnp.einsum("ihqk,ikhe->iqhe", d_scores, key_part, preferred_element_type=jnp.float32)
        * HEAD_DIM ** (-0.5)
    ).astype(jnp.bfloat16)
    d_keys = (
        jnp.einsum("ihqk,iqhe->ikhe", d_scores, queries, preferred_element_type=jnp.float32)
        * HEAD_DIM ** (-0.5)
    ).astype(jnp.bfloat16)
    d_projected = jnp.concatenate(
        [
            d_queries.reshape(images, slots, width),
            d_keys.reshape(images, slots, width),
            d_values.reshape(images, slots, width),
        ],
        axis=2,
    )
    grad_w_qkv = jnp.einsum("isd,ise->de", normed, d_projected, preferred_element_type=jnp.float32)
    grad_b_qv = jnp.concatenate(
        [
            jnp.sum(d_queries.astype(jnp.float32), axis=(0, 1)).reshape(width),
            jnp.sum(d_values.astype(jnp.float32), axis=(0, 1)).reshape(width),
        ]
    )
    d_normed = jnp.einsum("ise,de->isd", d_projected, qkv_full, preferred_element_type=jnp.float32)
    d_shift_one = jnp.sum(d_normed, axis=1)
    d_scale_one = jnp.sum(d_normed * norm_one, axis=1)
    unused_first, first_pull = jax.vjp(layer_norm, tokens_wide)
    grad_tokens = (d_middle + first_pull(d_normed * (1.0 + scale_one))[0]).astype(jnp.bfloat16)
    d_modulation = jnp.concatenate(
        [d_shift_one, d_scale_one, d_gate_one, d_shift_two, d_scale_two, d_gate_two], axis=1
    ).astype(jnp.bfloat16)
    grad_w_ada = jnp.einsum("id,ie->de", cond_act, d_modulation, preferred_element_type=jnp.float32)
    grad_b_ada = jnp.sum(d_modulation.astype(jnp.float32), axis=0)
    d_cond_act = jnp.einsum("ie,de->id", d_modulation, ada_full, preferred_element_type=jnp.float32)
    unused_silu, silu_pull = jax.vjp(lambda inner: inner * jax.nn.sigmoid(inner), cond_wide)
    grad_condition = silu_pull(d_cond_act)[0]
    narrow = (
        lax.psum_scatter(
            grad_w_ada.astype(jnp.bfloat16), "fsdp", scatter_dimension=0, tiled=True
        ).astype(jnp.float32),
        lax.psum_scatter(
            grad_w_qkv.astype(jnp.bfloat16), "fsdp", scatter_dimension=0, tiled=True
        ).astype(jnp.float32),
        lax.psum_scatter(
            grad_w_out.astype(jnp.bfloat16), "fsdp", scatter_dimension=0, tiled=True
        ).astype(jnp.float32),
        lax.psum_scatter(
            grad_w_up.astype(jnp.bfloat16), "fsdp", scatter_dimension=0, tiled=True
        ).astype(jnp.float32),
        lax.psum_scatter(
            grad_w_down.astype(jnp.bfloat16), "fsdp", scatter_dimension=0, tiled=True
        ).astype(jnp.float32),
        lax.psum_scatter(
            grad_b_ada.astype(jnp.bfloat16), "fsdp", scatter_dimension=0, tiled=True
        ).astype(jnp.float32),
        lax.psum_scatter(
            grad_b_qv.astype(jnp.bfloat16), "fsdp", scatter_dimension=0, tiled=True
        ).astype(jnp.float32),
        lax.psum_scatter(
            grad_b_out.astype(jnp.bfloat16), "fsdp", scatter_dimension=0, tiled=True
        ).astype(jnp.float32),
        lax.psum_scatter(
            grad_b_up.astype(jnp.bfloat16), "fsdp", scatter_dimension=0, tiled=True
        ).astype(jnp.float32),
        lax.psum_scatter(
            grad_b_down.astype(jnp.bfloat16), "fsdp", scatter_dimension=0, tiled=True
        ).astype(jnp.float32),
    )
    summed_weights = (
        lax.psum_scatter(narrow[0], "dp", scatter_dimension=1, tiled=True),
        lax.psum_scatter(narrow[1], "dp", scatter_dimension=1, tiled=True),
        lax.psum_scatter(narrow[2], "dp", scatter_dimension=1, tiled=True),
        lax.psum_scatter(narrow[3], "dp", scatter_dimension=1, tiled=True),
        lax.psum_scatter(narrow[4], "dp", scatter_dimension=1, tiled=True),
    )
    summed_biases = lax.psum((narrow[5], narrow[6], narrow[7], narrow[8], narrow[9]), "dp")
    return (
        output,
        grad_tokens,
        grad_condition,
        summed_weights[0],
        summed_weights[1],
        summed_weights[2],
        summed_weights[3],
        summed_weights[4],
        summed_biases[0],
        summed_biases[1],
        summed_biases[2],
        summed_biases[3],
        summed_biases[4],
    )


def solution(mesh):
    return jax.shard_map(
        body,
        mesh=mesh,
        in_specs=(
            P(("dp", "fsdp"), None, None),
            P(("dp", "fsdp"), None),
            P(("dp", "fsdp"), None),
            P("fsdp", None),
            P("fsdp", None),
            P("fsdp", None),
            P("fsdp", None),
            P("fsdp", None),
            P("fsdp"),
            P("fsdp"),
            P("fsdp"),
            P("fsdp"),
            P("fsdp"),
            P(("dp", "fsdp"), None, None),
        ),
        out_specs=(
            P(("dp", "fsdp"), None, None),
            P(("dp", "fsdp"), None, None),
            P(("dp", "fsdp"), None),
            P("fsdp", "dp"),
            P("fsdp", "dp"),
            P("fsdp", "dp"),
            P("fsdp", "dp"),
            P("fsdp", "dp"),
            P("fsdp"),
            P("fsdp"),
            P("fsdp"),
            P("fsdp"),
            P("fsdp"),
        ),
        check_vma=False,
    )
```

profile of v0, /device:TPU:0, one launch (start us, length us, event | category | flops | bytes accessed | tf_op | source)
XLA Modules:
  0.0 2053.4 jit_solution(9514321274415671537)
XLA Ops:
  14.4 21.8 %all-reduce.11 = (bf16[2304]{0:T(1024)(128)(2,1)S(1)}, bf16[6912]{0:T(1024)(128)(2,1)S(1)}, bf16[1152]{0:T(1024)(128)(2,1)S(1)}, bf16[1152]{0:T(1024)(128)(2,1)}) all-reduce(bf16[2304]{0:T(1024)(128)(2,1)S(1)} %dynamic-update-slice.1, bf16[6912]{0:T(1024)(128)(2,1)S(1)} %dynamic-update-slice, ...), channel_id=1, replica_groups=mesh['dp'=8,'fsdp'=4] {'fsdp'}, use_global_device_ids=true, to_apply=%add.1 | all-reduce | flops 11520 | bytes 46080
  36.8 17.0 all-gather
  58.1 227.6 %all-gather.7.cloned.1.call-done = bf16[1152,6912]{1,0:T(8,128)(2,1)} async-done(((bf16[288,6912]{1,0:T(8,128)(2,1)}), bf16[1152,6912]{1,0:T(8,128)(2,1)}) %all-gather.7.cloned.1.call-update) | async-done | bytes 15925264 | tf_op jit(solution)/shard_map/all_gather | solution.py:120
  285.7 7.7 convolution_reduce_fusion
  294.2 134.1 %all-gather.9.cloned.1.call-done = bf16[1152,3456]{1,0:T(8,128)(2,1)} async-done(((bf16[288,3456]{1,0:T(8,128)(2,1)}), bf16[1152,3456]{1,0:T(8,128)(2,1)}) %all-gather.9.cloned.1.call-update) | async-done | bytes 7962640 | tf_op jit(solution)/shard_map/all_gather | solution.py:121
  428.3 6.0 convolution_bitcast_fusion
  434.3 0.9 slice.46
  435.8 1.3 copy.53
  437.1 1.1 fusion.6
  438.3 1.0 exponential_reduce_fusion
  439.3 0.9 copy-done
  440.2 1.7 convolution_convert_fusion.6
  441.9 41.5 %all-gather.11.cloned.1.call-done = bf16[1152,1152]{1,0:T(8,128)(2,1)} async-done(((bf16[288,1152]{1,0:T(8,128)(2,1)}), bf16[1152,1152]{1,0:T(8,128)(2,1)}) %all-gather.11.cloned.1.call-update) | async-done | bytes 2654224 | tf_op jit(solution)/shard_map/all_gather | solution.py:122
  483.4 3.9 fusion.60
  489.3 180.4 %all-gather.13.cloned.1.call-done = bf16[1152,4608]{1,0:T(8,128)(2,1)} async-done(((bf16[288,4608]{1,0:T(8,128)(2,1)}), bf16[1152,4608]{1,0:T(8,128)(2,1)}) %all-gather.13.cloned.1.call-update) | async-done | bytes 10616848 | tf_op jit(solution)/shard_map/all_gather | solution.py:123
  669.7 9.3 convolution_add_fusion
  679.0 176.4 %all-gather.15.cloned.1.call-done = bf16[4608,1152]{1,0:T(8,128)(2,1)} async-done(((bf16[1152,1152]{1,0:T(8,128)(2,1)}), bf16[4608,1152]{1,0:T(8,128)(2,1)}) %all-gather.15.cloned.1.call-update) | async-done | bytes 10616848 | tf_op jit(solution)/shard_map/all_gather | solution.py:124
  855.4 10.1 fusion.64
  865.5 8.8 fusion.24
  874.8 1.0 copy-done.15
  875.8 1.0 fusion.58
  877.7 1.9 convolution_convert_fusion.4
  879.5 2.1 copy.55
  881.7 4.3 bitcast_reduce_fusion
  886.0 1.5 multiply_reduce_fusion
  887.5 1.4 multiply_convert_fusion.2
  889.7 1.2 bitcast_reduce_fusion.1
  891.7 5.8 convolution_convert_fusion.2
  898.2 8.7 convolution_convert_fusion.1
  907.0 1.4 convert_element_type.228
  908.4 1.3 convert.45
  910.3 7.0 fusion.20
  918.0 0.9 dynamic-update-slice.4
  919.6 1.9 fusion.18
  921.5 0.9 dynamic-update-slice.5
  923.1 11.8 fusion.23
  934.8 0.9 dynamic-update-slice.6
  935.7 0.9 dynamic-update-slice.7
  936.6 0.9 dynamic-update-slice.8
  937.4 0.9 dynamic-update-slice.9
  938.3 6.6 multiply_convert_fusion
  946.0 2.4 convolution_convert_fusion.3
  948.5 1.0 copy-done.16
  949.4 10.6 convolution_convert_fusion
  960.1 73.8 %reduce-scatter.23.cloned.1.call-done = bf16[288,3456]{1,0:T(8,128)(2,1)} async-done(((bf16[1152,3456]{1,0:T(8,128)(2,1)}), bf16[288,3456]{1,0:T(8,128)(2,1)}) %reduce-scatter.23.cloned.1.call-update) | async-done | bytes 1990672 | tf_op jit(solution)/shard_map/reduce_scatter | solution.py:253
  1034.0 4.5 copy.67
  1038.5 178.7 %reduce-scatter.27.cloned.1.call-done = bf16[288,4608]{1,0:T(8,128)(2,1)} async-done(((bf16[1152,4608]{1,0:T(8,128)(2,1)}), bf16[288,4608]{1,0:T(8,128)(2,1)}) %reduce-scatter.27.cloned.1.call-update) | async-done | bytes 2654224 | tf_op jit(solution)/shard_map/reduce_scatter | solution.py:259
  1217.2 5.5 copy.71
  1222.8 265.3 %reduce-scatter.21.cloned.1.call-done = bf16[288,6912]{1,0:T(8,128)(2,1)} async-done(((bf16[1152,6912]{1,0:T(8,128)(2,1)}), bf16[288,6912]{1,0:T(8,128)(2,1)}) %reduce-scatter.21.cloned.1.call-update) | async-done | bytes 3981328 | tf_op jit(solution)/shard_map/reduce_scatter | solution.py:250
  1488.1 7.7 copy.65
  1495.8 47.9 %reduce-scatter.25.cloned.1.call-done = bf16[288,1152]{1,0:T(8,128)(2,1)} async-done(((bf16[1152,1152]{1,0:T(8,128)(2,1)}), bf16[288,1152]{1,0:T(8,128)(2,1)}) %reduce-scatter.25.cloned.1.call-update) | async-done | bytes 663568 | tf_op jit(solution)/shard_map/reduce_scatter | solution.py:256
  1543.7 2.6 copy.69
  1546.4 179.5 %reduce-scatter.29.cloned.1.call-done = bf16[1152,1152]{1,0:T(8,128)(2,1)} async-done(((bf16[4608,1152]{1,0:T(8,128)(2,1)}), bf16[1152,1152]{1,0:T(8,128)(2,1)}) %reduce-scatter.29.cloned.1.call-update) | async-done | bytes 2654224 | tf_op jit(solution)/shard_map/reduce_scatter | solution.py:262
  1725.9 5.4 copy.73
  1734.2 19.1 all-reduce.10
  1753.7 23.5 %all-reduce.9 = (f32[1728]{0:T(1024)}, f32[576]{0:T(1024)}, f32[288]{0:T(512)}, f32[1152]{0:T(1024)}, f32[288]{0:T(512)}) all-reduce(f32[1728]{0:T(1024)S(1)} %dynamic-slice_convert_fusion.1, f32[576]{0:T(1024)S(1)} %dynamic-slice_convert_fusion.2, f32[288]{0:T(512)S(1)} %get-tuple-element.112, ...), channel_id=1, replica_groups=mesh['dp'=8,'fsdp'=4] {'dp'}, use_global_device_ids=true, to_apply=%region_28.29 | all-reduce | flops 4032 | bytes 32256 | tf_op jit(solution)/shard_map/psum | solution.py:288
  1777.1 10.4 fusion.40
  1787.7 2.1 copy.68
  1789.8 67.2 %reduce-scatter.37.cloned.1.call-done = f32[576,288]{1,0:T(8,128)} async-done(((f32[4608,288]{1,0:T(8,128)}), f32[576,288]{1,0:T(8,128)}) %reduce-scatter.37.cloned.1.call-update) | async-done | bytes 663568
  1857.0 2.3 copy.72
  1859.3 83.4 %reduce-scatter.31.cloned.1.call-done = f32[864,288]{1,0:T(8,128)} async-done(((f32[6912,288]{1,0:T(8,128)}), f32[864,288]{1,0:T(8,128)}) %reduce-scatter.31.cloned.1.call-update) | async-done | bytes 995344
  1942.7 2.7 copy.66
  1945.4 40.5 %reduce-scatter.35.cloned.1.call-done = f32[144,288]{1,0:T(8,128)} async-done(((f32[1152,288]{1,0:T(8,128)}), f32[144,288]{1,0:T(8,128)}) %reduce-scatter.35.cloned.1.call-update) | async-done | bytes 165904
  1985.9 60.8 %reduce-scatter.39.cloned.1.call-done = f32[144,1152]{1,0:T(8,128)} async-done(((f32[1152,1152]{1,0:T(8,128)}), f32[144,1152]{1,0:T(8,128)}) %reduce-scatter.39.cloned.1.call-update) | async-done | bytes 663568
  (202 shorter events, 20.5 us)
Async XLA Ops:
  7.2 278.5 %all-gather.7.cloned.1.call-start = ((), (), s32[]{:S(2)}) async-start(), calls=%async_computation.10 | async-start | bytes 19906560 | tf_op jit(solution)/shard_map/all_gather | solution.py:120
  7.9 420.3 %all-gather.9.cloned.1.call-start = ((), (), s32[]{:S(2)}) async-start(), calls=%async_computation.11 | async-start | bytes 9953280 | tf_op jit(solution)/shard_map/all_gather | solution.py:121
  8.7 474.8 %all-gather.11.cloned.1.call-start = ((), (), s32[]{:S(2)}) async-start(), calls=%async_computation.12 | async-start | bytes 3317760 | tf_op jit(solution)/shard_map/all_gather | solution.py:122
  9.4 1.3 copy-start.54
  9.4 3.9 copy-start.59
  9.4 4.1 copy-start.60
  9.4 4.4 copy-start.55
  9.4 4.6 copy-start.51
  9.5 27.4 %copy-start.52 = (bf16[1152]{0:T(1024)(128)(2,1)S(1)}, bf16[1152]{0:T(1024)(128)(2,1)}, u32[]{:S(2)}) copy-start(bf16[1152]{0:T(1024)(128)(2,1)} %param.25) | copy-start | bytes 6916
  9.5 45.0 %copy-start.56 = (s32[1,2]{1,0:T(1,128)S(1)}, s32[1,2]{1,0:T(1,128)}, u32[]{:S(2)}) copy-start(s32[1,2]{1,0:T(1,128)} %param.16) | copy-start | bytes 28
  9.5 47.5 %copy-start.2 = (bf16[1,256,1152]{2,1,0:T(8,128)(2,1)S(1)}, bf16[1,256,1152]{2,1,0:T(8,128)(2,1)}, u32[]{:S(2)}) copy-start(bf16[1,256,1152]{2,1,0:T(8,128)(2,1)} %param.14) | copy-start | bytes 1769476
  9.5 660.2 %all-gather.13.cloned.1.call-start = ((), (), s32[]{:S(2)}) async-start(), calls=%async_computation.13 | async-start | bytes 13271040 | tf_op jit(solution)/shard_map/all_gather | solution.py:123
  10.1 47.4 %copy-start.21 = (bf16[1,1152]{1,0:T(2,128)(2,1)S(1)}, bf16[1,1152]{1,0:T(2,128)(2,1)}, u32[]{:S(2)}) copy-start(bf16[1,1152]{1,0:T(2,128)(2,1)} %param.15) | copy-start | bytes 6916
  10.1 845.4 %all-gather.15.cloned.1.call-start = ((), (), s32[]{:S(2)}) async-start(), calls=%async_computation.14 | async-start | bytes 13271040 | tf_op jit(solution)/shard_map/all_gather | solution.py:124
  10.7 1023.3 %reduce-scatter.23.cloned.1.call-start = ((), (), s32[]{:S(2)}) async-start(), calls=%async_computation.16 | async-start | bytes 9953280 | tf_op jit(solution)/shard_map/reduce_scatter | solution.py:253
  56.4 381.9 %copy-start.47 = (pred[256]{0:T(512)(128)(4,1)}, pred[256]{0:T(512)(128)(4,1)S(1)}, u32[]{:S(2)}) copy-start(pred[256]{0:T(512)(128)(4,1)S(1)} %iota_compare_fusion) | copy-start | bytes 772
  57.1 371.1 %copy-start.38 = (f32[256]{0:T(256)}, f32[256]{0:T(256)S(1)}, u32[]{:S(2)}) copy-start(f32[256]{0:T(256)S(1)} %broadcast_multiply_fusion.1) | copy-start | bytes 3076
  57.4 236.0 %copy-start.42 = (f32[256]{0:T(256)}, f32[256]{0:T(256)S(1)}, u32[]{:S(2)}) copy-start(f32[256]{0:T(256)S(1)} %fusion.19) | copy-start | bytes 3076
  57.5 370.8 %copy-start.40 = (f32[256]{0:T(256)}, f32[256]{0:T(256)S(1)}, u32[]{:S(2)}) copy-start(f32[256]{0:T(256)S(1)} %fusion.45) | copy-start | bytes 3076
  58.1 235.3 %copy-start.23 = (f32[1,1152]{1,0:T(1,128)}, f32[1,1152]{1,0:T(1,128)S(1)}, u32[]{:S(2)}) copy-start(f32[1,1152]{1,0:T(1,128)S(1)} %get-tuple-element.81) | copy-start | bytes 13828
  294.2 140.1 %copy-start.27 = (f32[1152]{0:T(1024)}, f32[1152]{0:T(1024)S(1)}, u32[]{:S(2)}) copy-start(f32[1152]{0:T(1024)S(1)} %get-tuple-element.62) | copy-start | bytes 13828
  294.2 140.1 %copy-start.45 = (f32[1152]{0:T(1024)}, f32[1152]{0:T(1024)S(1)}, u32[]{:S(2)}) copy-start(f32[1152]{0:T(1024)S(1)} %get-tuple-element.61) | copy-start | bytes 13828
  435.6 3.7 copy-start.7
  438.3 2.0 copy-start
  855.4 10.1 copy-start.17
  855.4 10.1 copy-start.30
  855.4 10.1 copy-start.35
  865.5 8.8 copy-start.12
  865.5 8.9 copy-start.44
  874.3 2.5 copy-start.3
  874.3 1.5 copy-start.15
  874.3 1.5 copy-start.19
  874.3 1.5 copy-start.25
  874.4 1.5 copy-start.57
  874.4 3.3 copy-start.6
  874.8 2.1 copy-start.5
  874.8 2.0 copy-start.50
  881.7 4.3 copy-start.1
  881.7 4.3 copy-start.8
  881.7 4.3 copy-start.9
  881.7 4.3 copy-start.48
  886.0 4.9 copy-start.61
  889.6 2.1 copy-start.28
  889.6 2.1 copy-start.39
  889.6 2.1 copy-start.41
  889.7 2.1 copy-start.46
  897.6 319.6 %reduce-scatter.27.cloned.1.call-start = ((), (), s32[]{:S(2)}) async-start(), calls=%async_computation.18 | async-start | bytes 13271040 | tf_op jit(solution)/shard_map/reduce_scatter | solution.py:259
  906.9 2.7 copy-start.4
  907.0 581.1 %reduce-scatter.21.cloned.1.call-start = ((), (), s32[]{:S(2)}) async-start(), calls=%async_computation.15 | async-start | bytes 19906560 | tf_op jit(solution)/shard_map/reduce_scatter | solution.py:250
  919.6 1.9 copy-start.49
  944.9 598.8 %reduce-scatter.25.cloned.1.call-start = ((), (), s32[]{:S(2)}) async-start(), calls=%async_computation.17 | async-start | bytes 3317760 | tf_op jit(solution)/shard_map/reduce_scatter | solution.py:256
  948.4 777.5 %reduce-scatter.29.cloned.1.call-start = ((), (), s32[]{:S(2)}) async-start(), calls=%async_computation.19 | async-start | bytes 13271040 | tf_op jit(solution)/shard_map/reduce_scatter | solution.py:262
  960.1 827.6 %reduce-scatter.33.cloned.1.call-start = ((), (), s32[]{:S(2)}) async-start(), calls=%async_computation.21 | async-start | bytes 5971968
  1038.5 818.5 %reduce-scatter.37.cloned.1.call-start = ((), (), s32[]{:S(2)}) async-start(), calls=%async_computation.23 | async-start | bytes 7962624
  1222.7 720.0 %reduce-scatter.31.cloned.1.call-start = ((), (), s32[]{:S(2)}) async-start(), calls=%async_computation.20 | async-start | bytes 11943936
  1495.8 490.2 %reduce-scatter.35.cloned.1.call-start = ((), (), s32[]{:S(2)}) async-start(), calls=%async_computation.22 | async-start | bytes 1990656
  1546.4 500.3 %reduce-scatter.39.cloned.1.call-start = ((), (), s32[]{:S(2)}) async-start(), calls=%async_computation.24 | async-start | bytes 5971968
  1731.3 2.6 copy-start.53
  1731.3 2.7 copy-start.34
  1731.3 2.8 copy-start.32
  1731.3 2.9 copy-start.33
  1731.3 2.9 copy-start.37
  1731.3 45.8 %copy-start.22 = (bf16[1,1152]{1,0:T(2,128)(2,1)S(1)}, bf16[1,1152]{1,0:T(2,128)(2,1)}, u32[]{:S(2)}) copy-start(bf16[1,1152]{1,0:T(2,128)(2,1)} %param.15) | copy-start | bytes 6916
  1731.3 45.8 %copy-start.24 = (f32[1,1152]{1,0:T(1,128)S(1)}, f32[1,1152]{1,0:T(1,128)}, u32[]{:S(2)}) copy-start(f32[1,1152]{1,0:T(1,128)} %copy-done.23) | copy-start | bytes 13828
  (13 other events, 11.1 us)
Sparse Core Ops, SparseCore 0:
  9.6 276.1 all-gather.6
  287.3 140.9 all-gather.8
  429.8 53.5 all-gather.10
  484.9 184.8 all-gather.12
  671.1 184.2 all-gather.14
  897.7 136.2 reduce-scatter.22
  1036.5 180.6 reduce-scatter.26
  1219.6 268.4 reduce-scatter.20
  1490.5 53.2 reduce-scatter.24
  1546.1 179.7 reduce-scatter.28
  1729.3 58.3 reduce-scatter.32
  1791.5 65.4 reduce-scatter.36
  1860.5 82.1 reduce-scatter.30
  1946.5 39.4 reduce-scatter.34
  1989.8 56.9 reduce-scatter.38
where the time goes:
time: 2060 us; the launch traced here: 2050 us
  waiting for transfers between devices  1760 us (85%)
  matrix products  115 us (6%)
  blocking collectives  81.5 us (4%)
  local copies, waits for them, and re-layouts  52.8 us (3%)
  other arithmetic  22.1 us (1%)
    reduce_scatter x1, waiting for transfers between devices, body(): lax.psum_scatter(grad_w_ada.astype(jnp.bfloat16), 'fsdp', scatter_dimensi...  265 us
    unnamed x20, waiting for transfers between devices  255 us
    all_gather x1, waiting for transfers between devices, body(): lax.all_gather(w_ada, 'fsdp', axis=0, tiled=True)  228 us
    all_gather x1, waiting for transfers between devices, body(): lax.all_gather(w_up, 'fsdp', axis=0, tiled=True)  180 us
    reduce_scatter x1, waiting for transfers between devices, body(): lax.psum_scatter(grad_w_down.astype(jnp.bfloat16), 'fsdp', scatter_dimens...  179 us
    reduce_scatter x1, waiting for transfers between devices, body(): lax.psum_scatter(grad_w_up.astype(jnp.bfloat16), 'fsdp', scatter_dimensio...  179 us
    all_gather x1, waiting for transfers between devices, body(): lax.all_gather(w_down, 'fsdp', axis=0, tiled=True)  176 us
    all_gather x1, waiting for transfers between devices, body(): lax.all_gather(w_qkv, 'fsdp', axis=0, tiled=True)  134 us
  transfers between devices with their start and end apart: 15, of which 15 were waited for; matrix products, arithmetic and copies ran while one was open for 7% of the time, Pallas kernels for 0%

commit v1 on v0

--- a/solution.py
+++ b/solution.py
@@ -8,6 +8,18 @@
 epsilon = 1e-06
 masked_value = -1e30
 gelu_root = math.sqrt(2.0 / math.pi)
+
+
+def collect(x, axis, dim):
+    ways, here = (lax.axis_size(axis), lax.axis_index(axis))
+    grown, reach = (x, 1)
+    while reach < ways:
+        theirs = lax.ppermute(grown, axis, [(d, d ^ reach) for d in range(ways)])
+        mine_first = jnp.concatenate([grown, theirs], axis=dim)
+        theirs_first = jnp.concatenate([theirs, grown], axis=dim)
+        grown = jnp.where(here & reach == 0, mine_first, theirs_first)
+        reach = 2 * reach
+    return grown
 
 
 def layer_norm(values_in):
@@ -120,7 +132,7 @@
         lax.all_gather(w_ada, "fsdp", axis=0, tiled=True),
         lax.all_gather(w_qkv, "fsdp", axis=0, tiled=True),
         lax.all_gather(w_out, "fsdp", axis=0, tiled=True),
-        lax.all_gather(w_up, "fsdp", axis=0, tiled=True),
+        collect(w_up, "fsdp", 0),
         lax.all_gather(w_down, "fsdp", axis=0, tiled=True),
         lax.all_gather(b_ada, "fsdp", axis=0, tiled=True),
         lax.all_gather(b_qv, "fsdp", axis=0, tiled=True),

time: 2060 us -> 2100 us (1.019)
  blocking collectives: 81.5 us -> 297 us
  waiting for transfers between devices: 1760 us -> 1560 us
    unnamed x20, waiting for transfers between devices: 255 us -> 13.3 us
    unnamed x2, blocking collectives: 41 us -> 256 us
    reduce_scatter x1, waiting for transfers between devices: 47.9 us -> 87.8 us  [body(): lax.psum_scatter(grad_w_out.astype(jnp.bfloat16), 'fsdp', scatter_dimensi...]
    dot_general x4 -> x5, matrix products: 30.9 us -> 43.1 us  [apply_rows(): jnp.einsum('isd,de->ise', left, right, preferred_element_type=jnp.float32)]
    unnamed x147 -> x161, local copies, waits for them, and re-layouts: 45.7 us -> 49 us
  transfers between devices with their start and end apart: 15 -> 17, of which waited for: 15 -> 11; matrix products, arithmetic and copies ran while one was open for 7% -> 8% of each run, Pallas kernels for 0% -> 0%
where the time goes in v1:
time: 2100 us; the launch traced here: 2090 us
  waiting for transfers between devices  1560 us (74%)
  blocking collectives  297 us (14%)
  matrix products  123 us (6%)
  local copies, waits for them, and re-layouts  53.6 us (3%)
  other arithmetic  33.3 us (2%)
    reduce_scatter x1, waiting for transfers between devices, body(): lax.psum_scatter(grad_w_ada.astype(jnp.bfloat16), 'fsdp', scatter_dimensi...  265 us
    unnamed x2, blocking collectives  256 us
    all_gather x1, waiting for transfers between devices, body(): lax.all_gather(w_ada, 'fsdp', axis=0, tiled=True)  228 us
    reduce_scatter x1, waiting for transfers between devices, body(): lax.psum_scatter(grad_w_down.astype(jnp.bfloat16), 'fsdp', scatter_dimens...  184 us
    all_gather x1, waiting for transfers between devices, body(): lax.all_gather(w_up, 'fsdp', axis=0, tiled=True)  180 us
    reduce_scatter x1, waiting for transfers between devices, body(): lax.psum_scatter(grad_w_up.astype(jnp.bfloat16), 'fsdp', scatter_dimensio...  179 us
    all_gather x1, waiting for transfers between devices, body(): lax.all_gather(w_down, 'fsdp', axis=0, tiled=True)  176 us
    all_gather x1, waiting for transfers between devices, body(): lax.all_gather(w_qkv, 'fsdp', axis=0, tiled=True)  134 us
  transfers between devices with their start and end apart: 17, of which 11 were waited for; matrix products, arithmetic and copies ran while one was open for 8% of the time, Pallas kernels for 0%

profile of v1, /device:TPU:0, one launch (start us, length us, event | category | flops | bytes accessed | tf_op | source)
XLA Modules:
  0.0 2092.8 jit_solution(13971453054290381803)
XLA Ops:
  14.3 21.8 %all-reduce.11 = (bf16[2304]{0:T(1024)(128)(2,1)S(1)}, bf16[6912]{0:T(1024)(128)(2,1)S(1)}, bf16[1152]{0:T(1024)(128)(2,1)S(1)}, bf16[1152]{0:T(1024)(128)(2,1)}) all-reduce(bf16[2304]{0:T(1024)(128)(2,1)S(1)} %dynamic-update-slice.1, bf16[6912]{0:T(1024)(128)(2,1)S(1)} %dynamic-update-slice, ...), channel_id=1, replica_groups=mesh['dp'=8,'fsdp'=4] {'fsdp'}, use_global_device_ids=true, to_apply=%add.1 | all-reduce | flops 11520 | bytes 46080
  36.8 17.0 all-gather
  58.1 227.6 %all-gather.7.cloned.1.call-done = bf16[1152,6912]{1,0:T(8,128)(2,1)} async-done(((bf16[288,6912]{1,0:T(8,128)(2,1)}), bf16[1152,6912]{1,0:T(8,128)(2,1)}) %all-gather.7.cloned.1.call-update) | async-done | bytes 15925264 | tf_op jit(solution)/shard_map/all_gather | solution.py:132
  285.7 7.7 convolution_reduce_fusion
  294.2 134.1 %all-gather.9.cloned.1.call-done = bf16[1152,3456]{1,0:T(8,128)(2,1)} async-done(((bf16[288,3456]{1,0:T(8,128)(2,1)}), bf16[1152,3456]{1,0:T(8,128)(2,1)}) %all-gather.9.cloned.1.call-update) | async-done | bytes 7962640 | tf_op jit(solution)/shard_map/all_gather | solution.py:133
  428.3 6.0 convolution_bitcast_fusion
  435.3 1.1 fusion.20
  436.4 1.0 exponential_reduce_fusion
  437.4 1.1 copy-done
  438.5 1.8 convolution_convert_fusion.6
  440.3 43.1 %all-gather.11.cloned.1.call-done = bf16[1152,1152]{1,0:T(8,128)(2,1)} async-done(((bf16[288,1152]{1,0:T(8,128)(2,1)}), bf16[1152,1152]{1,0:T(8,128)(2,1)}) %all-gather.11.cloned.1.call-update) | async-done | bytes 2654224 | tf_op jit(solution)/shard_map/all_gather | solution.py:134
  483.4 3.9 fusion.93
  489.3 180.4 %all-gather.15.cloned.1.call-done = bf16[1152,4608]{1,0:T(8,128)(2,1)} async-done(((bf16[288,4608]{1,0:T(8,128)(2,1)}), bf16[1152,4608]{1,0:T(8,128)(2,1)}) %all-gather.15.cloned.1.call-update) | async-done | bytes 10616848 | tf_op jit(solution)/shard_map/all_gather | solution.py:162
  669.7 9.5 convolution_add_fusion
  679.2 176.2 %all-gather.13.cloned.1.call-done = bf16[4608,1152]{1,0:T(8,128)(2,1)} async-done(((bf16[1152,1152]{1,0:T(8,128)(2,1)}), bf16[4608,1152]{1,0:T(8,128)(2,1)}) %all-gather.13.cloned.1.call-update) | async-done | bytes 10616848 | tf_op jit(solution)/shard_map/all_gather | solution.py:136
  855.4 10.2 fusion.97
  865.7 3.9 fusion.51
  870.1 1.0 copy-done.3
  871.1 1.1 fusion.91
  872.2 0.8 copy-done.11
  873.0 1.8 convolution_convert_fusion.4
  874.8 2.1 copy.55
  877.0 4.2 multiply_reduce_fusion
  881.2 1.9 bitcast_reduce_fusion
  883.1 1.4 multiply_convert_fusion.2
  884.5 1.2 bitcast_reduce_fusion.1
  886.5 5.7 convolution_convert_fusion.2
  893.0 8.8 convolution_convert_fusion.1
  901.8 1.3 convert_element_type.231
  903.2 1.3 convert.45
  905.1 7.0 fusion.48
  912.8 1.5 dynamic-update-slice.4
  915.6 1.9 fusion.46
  917.5 1.5 dynamic-update-slice.5
  919.6 3.9 fusion.52
  923.5 1.5 dynamic-update-slice.6
  925.0 1.5 dynamic-update-slice.7
  926.5 1.4 dynamic-update-slice.8
  927.9 9.0 fusion.43
  937.3 5.9 multiply_convert_fusion
  943.2 1.0 copy-done.12
  944.2 2.5 convolution_convert_fusion.3
  947.0 0.8 copy-done.10
  947.8 10.7 convolution_convert_fusion
  958.6 70.2 %reduce-scatter.23.cloned.1.call-done = bf16[288,3456]{1,0:T(8,128)(2,1)} async-done(((bf16[1152,3456]{1,0:T(8,128)(2,1)}), bf16[288,3456]{1,0:T(8,128)(2,1)}) %reduce-scatter.23.cloned.1.call-update) | async-done | bytes 1990672 | tf_op jit(solution)/shard_map/reduce_scatter | solution.py:265
  1028.7 4.5 copy.67
  1033.3 178.6 %reduce-scatter.27.cloned.1.call-done = bf16[288,4608]{1,0:T(8,128)(2,1)} async-done(((bf16[1152,4608]{1,0:T(8,128)(2,1)}), bf16[288,4608]{1,0:T(8,128)(2,1)}) %reduce-scatter.27.cloned.1.call-update) | async-done | bytes 2654224 | tf_op jit(solution)/shard_map/reduce_scatter | solution.py:271
  1211.9 5.5 copy.71
  1217.5 265.3 %reduce-scatter.21.cloned.1.call-done = bf16[288,6912]{1,0:T(8,128)(2,1)} async-done(((bf16[1152,6912]{1,0:T(8,128)(2,1)}), bf16[288,6912]{1,0:T(8,128)(2,1)}) %reduce-scatter.21.cloned.1.call-update) | async-done | bytes 3981328 | tf_op jit(solution)/shard_map/reduce_scatter | solution.py:262
  1482.8 7.7 copy.65
  1490.6 87.8 %reduce-scatter.25.cloned.1.call-done = bf16[288,1152]{1,0:T(8,128)(2,1)} async-done(((bf16[1152,1152]{1,0:T(8,128)(2,1)}), bf16[288,1152]{1,0:T(8,128)(2,1)}) %reduce-scatter.25.cloned.1.call-update) | async-done | bytes 663568 | tf_op jit(solution)/shard_map/reduce_scatter | solution.py:268
  1578.4 2.7 copy.69
  1581.1 183.6 %reduce-scatter.29.cloned.1.call-done = bf16[1152,1152]{1,0:T(8,128)(2,1)} async-done(((bf16[4608,1152]{1,0:T(8,128)(2,1)}), bf16[1152,1152]{1,0:T(8,128)(2,1)}) %reduce-scatter.29.cloned.1.call-update) | async-done | bytes 2654224 | tf_op jit(solution)/shard_map/reduce_scatter | solution.py:274
  1764.8 5.4 copy.73
  1770.3 8.0 maximum_select_fusion.4
  1778.3 4.2 collective-permute-start.1
  1785.1 234.6 %all-reduce.10 = (bf16[6912]{0:T(1024)(128)(2,1)S(1)}, bf16[2304]{0:T(1024)(128)(2,1)S(1)}, bf16[1152]{0:T(1024)(128)(2,1)S(1)}, bf16[4608]{0:T(1024)(128)(2,1)S(1)}, bf16[1152]{0:T(1024)(128)(2,1)S(1)}) all-reduce(bf16[6912]{0:T(1024)(128)(2,1)S(1)} %dynamic-update-slice.9, ...), channel_id=12, replica_groups=mesh['dp'=8,'fsdp'=4] {'fsdp'}, use_global_device_ids=true, to_apply=%region_27.28.clone | all-reduce | flops 16128 | bytes 64512
  2020.0 23.4 %all-reduce.9 = (f32[1728]{0:T(1024)}, f32[576]{0:T(1024)}, f32[288]{0:T(512)}, f32[1152]{0:T(1024)}, f32[288]{0:T(512)}) all-reduce(f32[1728]{0:T(1024)S(1)} %dynamic-slice_convert_fusion.1, f32[576]{0:T(1024)S(1)} %dynamic-slice_convert_fusion.2, f32[288]{0:T(512)S(1)} %get-tuple-element.110, ...), channel_id=1, replica_groups=mesh['dp'=8,'fsdp'=4] {'dp'}, use_global_device_ids=true, to_apply=%region_28.29 | all-reduce | flops 4032 | bytes 32256 | tf_op jit(solution)/shard_map/psum | solution.py:300
  2043.5 10.4 fusion.65
  2054.0 14.7 fusion.28
  2068.7 2.1 copy.68
  2070.8 2.3 copy.72
  2073.2 2.7 copy.66
  2075.9 10.0 reduce-scatter.39.cloned.1.call-done
  (223 shorter events, 19.2 us)
Async XLA Ops:
  7.2 278.5 %all-gather.7.cloned.1.call-start = ((), (), s32[]{:S(2)}) async-start(), calls=%async_computation.10 | async-start | bytes 19906560 | tf_op jit(solution)/shard_map/all_gather | solution.py:132
  7.9 420.3 %all-gather.9.cloned.1.call-start = ((), (), s32[]{:S(2)}) async-start(), calls=%async_computation.11 | async-start | bytes 9953280 | tf_op jit(solution)/shard_map/all_gather | solution.py:133
  8.7 474.8 %all-gather.11.cloned.1.call-start = ((), (), s32[]{:S(2)}) async-start(), calls=%async_computation.12 | async-start | bytes 3317760 | tf_op jit(solution)/shard_map/all_gather | solution.py:134
  9.4 3.9 copy-start.65
  9.4 4.1 copy-start.66
  9.4 4.4 copy-start.59
  9.4 4.7 copy-start.63
  9.5 27.3 %copy-start.60 = (bf16[1152]{0:T(1024)(128)(2,1)S(1)}, bf16[1152]{0:T(1024)(128)(2,1)}, u32[]{:S(2)}) copy-start(bf16[1152]{0:T(1024)(128)(2,1)} %param.25) | copy-start | bytes 6916
  9.5 45.0 %copy-start.64 = (s32[1,2]{1,0:T(1,128)S(1)}, s32[1,2]{1,0:T(1,128)}, u32[]{:S(2)}) copy-start(s32[1,2]{1,0:T(1,128)} %param.16) | copy-start | bytes 28
  9.5 47.5 %copy-start.2 = (bf16[1,256,1152]{2,1,0:T(8,128)(2,1)S(1)}, bf16[1,256,1152]{2,1,0:T(8,128)(2,1)}, u32[]{:S(2)}) copy-start(bf16[1,256,1152]{2,1,0:T(8,128)(2,1)} %param.14) | copy-start | bytes 1769476
  9.5 660.2 %all-gather.15.cloned.1.call-start = ((), (), s32[]{:S(2)}) async-start(), calls=%async_computation.14 | async-start | bytes 13271040 | tf_op jit(solution)/shard_map/all_gather | solution.py:162
  10.1 47.4 %copy-start.24 = (bf16[1,1152]{1,0:T(2,128)(2,1)S(1)}, bf16[1,1152]{1,0:T(2,128)(2,1)}, u32[]{:S(2)}) copy-start(bf16[1,1152]{1,0:T(2,128)(2,1)} %param.15) | copy-start | bytes 6916
  10.1 845.3 %all-gather.13.cloned.1.call-start = ((), (), s32[]{:S(2)}) async-start(), calls=%async_computation.13 | async-start | bytes 13271040 | tf_op jit(solution)/shard_map/all_gather | solution.py:136
  10.7 1018.0 %reduce-scatter.23.cloned.1.call-start = ((), (), s32[]{:S(2)}) async-start(), calls=%async_computation.16 | async-start | bytes 9953280 | tf_op jit(solution)/shard_map/reduce_scatter | solution.py:265
  56.4 380.0 %copy-start.55 = (pred[256]{0:T(512)(128)(4,1)}, pred[256]{0:T(512)(128)(4,1)S(1)}, u32[]{:S(2)}) copy-start(pred[256]{0:T(512)(128)(4,1)S(1)} %iota_compare_fusion) | copy-start | bytes 772
  57.1 371.1 %copy-start.36 = (f32[256]{0:T(256)}, f32[256]{0:T(256)S(1)}, u32[]{:S(2)}) copy-start(f32[256]{0:T(256)S(1)} %broadcast_multiply_fusion.1) | copy-start | bytes 3076
  57.4 228.3 %copy-start.49 = (f32[256]{0:T(256)}, f32[256]{0:T(256)S(1)}, u32[]{:S(2)}) copy-start(f32[256]{0:T(256)S(1)} %fusion.47) | copy-start | bytes 3076
  57.5 370.8 %copy-start.38 = (f32[256]{0:T(256)}, f32[256]{0:T(256)S(1)}, u32[]{:S(2)}) copy-start(f32[256]{0:T(256)S(1)} %fusion.70) | copy-start | bytes 3076
  58.1 235.3 %copy-start.26 = (f32[1,1152]{1,0:T(1,128)}, f32[1,1152]{1,0:T(1,128)S(1)}, u32[]{:S(2)}) copy-start(f32[1,1152]{1,0:T(1,128)S(1)} %get-tuple-element.79) | copy-start | bytes 13828
  294.2 140.1 %copy-start.19 = (f32[1152]{0:T(1024)}, f32[1152]{0:T(1024)S(1)}, u32[]{:S(2)}) copy-start(f32[1152]{0:T(1024)S(1)} %get-tuple-element.60) | copy-start | bytes 13828
  294.2 140.1 %copy-start.52 = (f32[1152]{0:T(1024)}, f32[1152]{0:T(1024)S(1)}, u32[]{:S(2)}) copy-start(f32[1152]{0:T(1024)S(1)} %get-tuple-element.59) | copy-start | bytes 13828
  435.3 2.1 copy-start.7
  436.4 2.1 copy-start
  855.4 10.2 copy-start.16
  855.4 10.2 copy-start.32
  855.4 10.2 copy-start.43
  855.4 10.2 copy-start.67
  865.6 3.9 copy-start.13
  865.6 3.9 copy-start.51
  869.5 2.6 copy-start.4
  869.6 3.4 copy-start.6
  870.0 2.1 copy-start.48
  877.0 4.2 copy-start.1
  877.0 4.2 copy-start.8
  877.0 4.3 copy-start.56
  883.1 3.4 copy-start.68
  884.4 2.1 copy-start.20
  886.5 5.8 copy-start.15
  892.3 319.6 %reduce-scatter.27.cloned.1.call-start = ((), (), s32[]{:S(2)}) async-start(), calls=%async_computation.18 | async-start | bytes 13271040 | tf_op jit(solution)/shard_map/reduce_scatter | solution.py:271
  901.7 2.7 copy-start.5
  901.8 581.0 %reduce-scatter.21.cloned.1.call-start = ((), (), s32[]{:S(2)}) async-start(), calls=%async_computation.15 | async-start | bytes 19906560 | tf_op jit(solution)/shard_map/reduce_scatter | solution.py:262
  927.9 9.0 copy-start.18
  927.9 9.3 copy-start.30
  943.2 635.2 %reduce-scatter.25.cloned.1.call-start = ((), (), s32[]{:S(2)}) async-start(), calls=%async_computation.17 | async-start | bytes 3317760 | tf_op jit(solution)/shard_map/reduce_scatter | solution.py:268
  946.7 818.0 %reduce-scatter.29.cloned.1.call-start = ((), (), s32[]{:S(2)}) async-start(), calls=%async_computation.19 | async-start | bytes 13271040 | tf_op jit(solution)/shard_map/reduce_scatter | solution.py:274
  958.5 1110.2 %reduce-scatter.33.cloned.1.call-start = ((), (), s32[]{:S(2)}) async-start(), calls=%async_computation.21 | async-start | bytes 5971968
  1033.2 1037.6 %reduce-scatter.37.cloned.1.call-start = ((), (), s32[]{:S(2)}) async-start(), calls=%async_computation.23 | async-start | bytes 7962624
  1217.4 855.7 %reduce-scatter.31.cloned.1.call-start = ((), (), s32[]{:S(2)}) async-start(), calls=%async_computation.20 | async-start | bytes 11943936
  1490.5 585.4 %reduce-scatter.35.cloned.1.call-start = ((), (), s32[]{:S(2)}) async-start(), calls=%async_computation.22 | async-start | bytes 1990656
  1490.6 279.7 %collective-permute-start = (bf16[288,4608]{1,0:T(8,128)(2,1)}, bf16[288,4608]{1,0:T(8,128)(2,1)}, u32[]{:S(2)}, u32[]{:S(2)}) collective-permute-start(bf16[288,4608]{1,0:T(8,128)(2,1)} %param.20), channel_id=1, source_target_pairs={{0,1},{1,0},{2,3},{3,2},{4,5},{5,4},{6,7},{7,6},{8,9},{9,8},{10,11... | collective-permute-start | bytes 7962632 | tf_op jit(solution)/shard_map/ppermute | solution.py:17
  1581.1 504.8 %reduce-scatter.39.cloned.1.call-start = ((), (), s32[]{:S(2)}) async-start(), calls=%async_computation.24 | async-start | bytes 5971968
  1770.2 14.6 copy-start.42
  1770.2 14.7 copy-start.61
  1770.2 14.8 copy-start.40
  1770.2 14.8 copy-start.41
  1770.2 14.8 copy-start.46
  1770.2 273.2 %copy-start.25 = (bf16[1,1152]{1,0:T(2,128)(2,1)S(1)}, bf16[1,1152]{1,0:T(2,128)(2,1)}, u32[]{:S(2)}) copy-start(bf16[1,1152]{1,0:T(2,128)(2,1)} %param.15) | copy-start | bytes 6916
  1770.3 273.2 %copy-start.27 = (f32[1,1152]{1,0:T(1,128)S(1)}, f32[1,1152]{1,0:T(1,128)}, u32[]{:S(2)}) copy-start(f32[1,1152]{1,0:T(1,128)} %copy-done.26) | copy-start | bytes 13828
  1778.3 275.6 %collective-permute-start.1 = (bf16[576,4608]{1,0:T(8,128)(2,1)}, bf16[576,4608]{1,0:T(8,128)(2,1)}, u32[]{:S(2)}, u32[]{:S(2)}) collective-permute-start(bf16[576,4608]{1,0:T(8,128)(2,1)} %maximum_select_fusion.4), channel_id=1, source_target_pairs={{0,2},{1,3},{2,0},{3,1},{4,6},{5,7},{6,4},{7,5},{8,10},{9,11},{10,... | collective-permute-start | bytes 15925256 | tf_op jit(solution)/shard_map/ppermute | solution.py:17
  2043.4 10.5 copy-start.23
  2043.4 10.5 copy-start.34
  2043.4 10.5 copy-start.35
  2043.5 10.5 copy-start.45
  2043.5 10.5 copy-start.54
  (22 other events, 25.3 us)
Sparse Core Ops, SparseCore 0:
  9.6 276.1 all-gather.6
  287.3 140.9 all-gather.8
  429.8 53.5 all-gather.10
  484.9 184.8 all-gather.14
  671.1 184.2 all-gather.12
  892.4 136.2 reduce-scatter.22
  1031.2 180.6 reduce-scatter.26
  1214.3 268.4 reduce-scatter.20
  1485.2 93.1 reduce-scatter.24
  1580.7 183.9 reduce-scatter.28
  1768.2 58.5 reduce-scatter.32
  1830.6 65.4 reduce-scatter.36
  1899.6 82.1 reduce-scatter.30
  1985.6 39.4 reduce-scatter.34
  2028.9 56.9 reduce-scatter.38
